TPU v7x, 512 devices: a whole 4x8x8 slice. The times are simulated.
512 devices in a mesh: dp: 64 (over z_lo, y, core), expert: 8 (over x, z_hi).
Axes of the slice: x: 4, y: 8, z: 8 (z_hi: 2, z_lo: 4; z = z_hi * 4 + z_lo), core: 2. Of those that a mesh axis runs over, the one named last changes fastest.
Arguments:
- tokens: bfloat16 [131072, 1024], P(('dp', 'expert')), may hold values from -6 to 6
- expert_ids: int32 [131072], P(('dp', 'expert')), may hold values from 0 to 7
- slots: int32 [131072], P(('dp', 'expert')), may hold values from -1 to 39, as said below
- router: bfloat16 [1024, 8], replicated, may hold values from -0.1875 to 0.1875
- w_in: bfloat16 [8, 1024, 2048], P('expert', 'dp'), may hold values from -0.1875 to 0.1875
- w_out: bfloat16 [8, 2048, 1024], P('expert', None, 'dp'), may hold values from -0.125 to 0.125
- texts: bfloat16 [2048, 1024], P(('dp', 'expert')), may hold values from -6 to 6
Outputs:
- d_tokens: bfloat16 [131072, 1024], P(('dp', 'expert'))
- d_texts: float32 [2048, 1024], P(('dp', 'expert'))
- router_grad: float32 [1024, 8], replicated
Inputs may be any that keep to these rules, and one draw needn't show every extreme that they name: Within each block of 256 tokens (one device's), the tokens of each expert hold slots 0, 1, 2, ... in token order until 40, and -1 after. On every index of dp, some expert receives all 40 slots from each of the 8 blocks of that index.
All inputs are finite; a program needn't handle non-finite values.
Results may differ from a plain program's by a relative error of at most 0.0064.
Values may be sent and summed in bfloat16 or wider, within the bound.
No kernel may reach another device: no remote copies, remote signals or barrier semaphores. Data moves between devices by JAX's collectives and lax.ppermute only.
A program may use at most 64 MiB of HBM per device.

v0:
```python
import jax
import jax.numpy as jnp
from jax import lax
from jax.sharding import PartitionSpec as P

highest = lax.Precision.HIGHEST
temper = 10.0
offset = -2.0
loss_scale = 256.0
epsilon = 1e-06


def shifted(block, axis, distance):
    devices = range(lax.axis_size(axis))
    route = [((i - distance) % len(devices), i) for i in devices]
    return lax.ppermute(block, axis, route)


def gelu_slope(hidden):
    result, pullback = jax.vjp(lambda inputs: jax.nn.gelu(inputs, approximate=True), hidden)
    return pullback(jnp.ones_like(hidden))[0]


def contract_last(left, right):
    return lax.dot_general(
        left, right, (((1,), (1,)), ((), ())), preferred_element_type=jnp.float32
    )


def unit_rows(matrix):
    values_float = matrix.astype(jnp.float32)
    scales = lax.rsqrt(jnp.sum(values_float * values_float, axis=1, keepdims=True) + epsilon)
    return (values_float * scales, scales)


def body(tokens, expert_ids, slots, router, w_in, w_out, texts):
    tok_count, model_width = tokens.shape
    experts = router.shape[1]
    capacity = 5 * tok_count // (4 * experts)
    images = texts.shape[0]
    patch_len = tok_count // images
    is_kept = slots >= 0
    kept_float = is_kept.astype(jnp.float32)
    columns = jnp.arange(experts, dtype=jnp.int32)
    chosen = (expert_ids[:, None] == columns[None, :]).astype(jnp.float32)
    logits = jnp.dot(tokens, router, preferred_element_type=jnp.float32)
    gate_values = jax.nn.sigmoid(jnp.sum(logits * chosen, axis=1))
    slot_total = experts * capacity
    places = jnp.where(is_kept, expert_ids * capacity + slots, slot_total)
    safe_places = jnp.minimum(places, slot_total - 1)
    send_buffer = (
        jnp.zeros((slot_total, model_width), jnp.bfloat16).at[places].set(tokens, mode="drop")
    )
    arrived = lax.all_to_all(
        send_buffer.reshape(experts, capacity, model_width),
        "expert",
        split_axis=0,
        concat_axis=0,
        tiled=True,
    )
    sources = arrived.shape[0]
    routed = arrived.reshape(sources * capacity, model_width)
    row_count = routed.shape[0]
    in_full, out_full = (
        lax.all_gather(w_in, "dp", axis=1, tiled=True),
        lax.all_gather(w_out, "dp", axis=2, tiled=True),
    )
    in_matrix = in_full[0]
    out_matrix = out_full[0]
    hidden = jnp.dot(routed, in_matrix, preferred_element_type=jnp.float32)
    active = jax.nn.gelu(hidden, approximate=True).astype(jnp.bfloat16)
    expert_out = jnp.dot(active, out_matrix, preferred_element_type=jnp.float32).astype(
        jnp.bfloat16
    )
    returned_rows = lax.all_to_all(
        expert_out.reshape(sources, capacity, model_width),
        "expert",
        split_axis=0,
        concat_axis=0,
        tiled=True,
    )
    combined = jnp.where(
        is_kept[:, None],
        returned_rows.reshape(slot_total, model_width)[safe_places].astype(jnp.float32),
        0.0,
    )
    branch = gate_values[:, None] * combined
    pooled = jnp.mean(branch.reshape(images, patch_len, model_width), axis=1)
    unit_img, pooled_scale = unit_rows(pooled)
    neighbour = shifted(texts, "dp", 1)
    own_unit, own_scale = unit_rows(texts)
    next_unit, unused = unit_rows(neighbour)
    diagonal = jnp.eye(images, dtype=jnp.float32)
    own_scores = temper * jnp.dot(unit_img, own_unit.T, precision=highest) + offset
    next_scores = temper * jnp.dot(unit_img, next_unit.T, precision=highest) + offset
    own_grad = loss_scale * (jax.nn.sigmoid(own_scores) - diagonal)
    next_grad = loss_scale * jax.nn.sigmoid(next_scores)
    grad_image = temper * (
        jnp.dot(own_grad, own_unit, precision=highest)
        + jnp.dot(next_grad, next_unit, precision=highest)
    )
    grad_text_own = temper * jnp.dot(own_grad.T, unit_img, precision=highest)
    grad_text_next = temper * jnp.dot(next_grad.T, unit_img, precision=highest)
    grad_text_back = shifted(grad_text_next, "dp", -1)
    grad_text = grad_text_own + grad_text_back
    d_texts = (
        grad_text - own_unit * jnp.sum(own_unit * grad_text, axis=1, keepdims=True)
    ) * own_scale
    grad_pooled = (
        grad_image - unit_img * jnp.sum(unit_img * grad_image, axis=1, keepdims=True)
    ) * pooled_scale
    grad_branch = jnp.broadcast_to(
        grad_pooled[:, None, :] / patch_len, (images, patch_len, model_width)
    ).reshape(tok_count, model_width)
    grad_combined = (gate_values[:, None] * grad_branch).astype(jnp.bfloat16)
    grad_buffer = (
        jnp.zeros((slot_total, model_width), jnp.bfloat16)
        .at[places]
        .set(grad_combined, mode="drop")
    )
    grad_gate = jnp.sum(grad_branch * combined, axis=1)
    grad_logits = chosen * (grad_gate * gate_values * (1.0 - gate_values) * kept_float)[:, None]
    partial_value = jnp.dot(tokens.astype(jnp.float32).T, grad_logits, precision=highest)
    router_grad = lax.psum(partial_value, ("dp", "expert"))
    router_part = jnp.dot(grad_logits, router.astype(jnp.float32).T, precision=highest)
    grads_in = lax.all_to_all(
        grad_buffer.reshape(experts, capacity, model_width),
        "expert",
        split_axis=0,
        concat_axis=0,
        tiled=True,
    )
    grads_in = grads_in.reshape(row_count, model_width)
    slopes = gelu_slope(hidden)
    grad_hidden = (contract_last(grads_in, out_matrix) * slopes).astype(jnp.bfloat16)
    grad_routed = contract_last(grad_hidden, in_matrix).astype(jnp.bfloat16)
    grad_back = lax.all_to_all(
        grad_routed.reshape(sources, capacity, model_width),
        "expert",
        split_axis=0,
        concat_axis=0,
        tiled=True,
    )
    grad_tokens = jnp.where(
        is_kept[:, None],
        grad_back.reshape(slot_total, model_width)[safe_places].astype(jnp.float32),
        0.0,
    )
    d_tokens = (grad_tokens + router_part).astype(jnp.bfloat16)
    return (d_tokens, d_texts, router_grad)


def solution(mesh):
    in_specs = (
        P(("dp", "expert"), None),
        P(("dp", "expert")),
        P(("dp", "expert")),
        P(),
        P("expert", "dp", None),
        P("expert", None, "dp"),
        P(("dp", "expert"), None),
    )
    out_specs = (P(("dp", "expert"), None), P(("dp", "expert"), None), P())
    return jax.shard_map(body, mesh=mesh, in_specs=in_specs, out_specs=out_specs, check_vma=False)
```

profile of v0, /device:TPU:1, one launch (start us, length us, event | category | flops | bytes accessed | tf_op | source)
XLA Modules:
  0.0 448.0 jit_solution(9497182288706210727)
XLA Ops:
  7.2 0.7 all-gather.3.cloned.1.call-update
  8.0 0.7 all-gather.5.cloned.1.call-update
  8.7 0.7 compare_select_fusion
  9.4 3.1 scatter_custom_fusion
  12.5 13.3 %all-to-all-start = ((bf16[8,40,1024]{2,1,0:T(8,128)(2,1)}), bf16[8,40,1024]{2,1,0:T(8,128)(2,1)S(1)}, u32[]{:S(2)}, u32[]{:S(2)}) async-start(bf16[8,40,1024]{2,1,0:T(8,128)(2,1)} %bitcast), calls=%async_computation | async-start | bytes 1310720 | tf_op jit(solution)/shard_map/all_to_all | solution.py:54
  25.7 4.0 collective-permute-start
  29.8 1.3 fusion.33
  31.1 10.3 %all-to-all-done = bf16[8,40,1024]{2,1,0:T(8,128)(2,1)S(1)} async-done(((bf16[8,40,1024]{2,1,0:T(8,128)(2,1)}), bf16[8,40,1024]{2,1,0:T(8,128)(2,1)S(1)}, u32[]{:S(2)}, u32[]{:S(2)}) %all-to-all-start) | async-done | bytes 655392 | tf_op jit(solution)/shard_map/all_to_all | solution.py:54
  41.4 98.3 %all-gather.3.cloned.1.call-done = bf16[1,1024,2048]{2,1,0:T(8,128)(2,1)} async-done(((bf16[1,16,2048]{2,1,0:T(8,128)(2,1)}), bf16[1,1024,2048]{2,1,0:T(8,128)(2,1)}) %all-gather.3.cloned.1.call-update) | async-done | bytes 4194320 | tf_op jit(solution)/shard_map/all_gather | solution.py:65
  139.6 3.7 fusion.6
  143.4 119.5 %all-gather.5.cloned.1.call-done = bf16[1,2048,1024]{1,2,0:T(8,128)(2,1)} async-done(((bf16[1,2048,16]{1,2,0:T(8,128)(2,1)}), bf16[1,2048,1024]{1,2,0:T(8,128)(2,1)}) %all-gather.5.cloned.1.call-update) | async-done | bytes 4194320 | tf_op jit(solution)/shard_map/all_gather | solution.py:66
  262.9 4.9 %fusion.23 = bf16[320,1024]{1,0:T(8,128)(2,1)} fusion(bf16[1,2048,1024]{1,2,0:T(8,128)(2,1)} %all-gather.5.cloned.1.call-done, f32[320,2048]{1,0:T(8,128)S(1)} %fusion.6), kind=kOutput, calls=%fused_computation.27 | convolution fusion | flops 1348403200 | bytes 7471104 | tf_op jit(solution)/shard_map/dot_general | solution.py:72
  267.8 7.5 %all-to-all-start.1 = ((bf16[8,40,1024]{2,1,0:T(8,128)(2,1)}), bf16[8,40,1024]{2,1,0:T(8,128)(2,1)S(1)}, u32[]{:S(2)}, u32[]{:S(2)}) async-start(bf16[8,40,1024]{2,1,0:T(8,128)(2,1)} %bitcast.4), calls=%async_computation.1 | async-start | bytes 1310720 | tf_op jit(solution)/shard_map/all_to_all | solution.py:75
  275.7 15.6 %all-to-all-done.1 = bf16[8,40,1024]{2,1,0:T(8,128)(2,1)S(1)} async-done(((bf16[8,40,1024]{2,1,0:T(8,128)(2,1)}), bf16[8,40,1024]{2,1,0:T(8,128)(2,1)S(1)}, u32[]{:S(2)}, u32[]{:S(2)}) %all-to-all-start.1) | async-done | bytes 655392 | tf_op jit(solution)/shard_map/all_to_all | solution.py:75
  291.4 1.2 gather_fusion
  294.5 1.9 scatter_custom_fusion.1
  296.3 14.7 %all_to_all.20 = bf16[8,40,1024]{2,1,0:T(8,128)(2,1)S(1)} all-to-all(bf16[8,40,1024]{2,1,0:T(8,128)(2,1)S(1)} %bitcast.51), channel_id=1, replica_groups=mesh['dp'=64,'expert'=8] {'expert'}, dimensions={0} | all-to-all | bytes 1310720 | tf_op jit(solution)/shard_map/all_to_all | solution.py:126
  311.1 8.7 %fusion.20 = bf16[320,1024]{1,0:T(8,128)(2,1)} fusion(bf16[1,1024,2048]{2,1,0:T(8,128)(2,1)} %all-gather.3.cloned.1.call-done, bf16[320,1024]{1,0:T(8,128)(2,1)S(1)} %bitcast.53, bf16[1,2048,1024]{1,2,0:T(8,128)(2,1)} %all-gather.5.cloned.1.call-done, f32[320,2048]{1,0:T(8,128)} %copy-done.5), kind=kOutput, calls=%fused_computation.26 | convolution fusion | flops 2697134080 | bytes 12320768 | tf_op jit(solution)/shard_map/dot_general | solution.py:25
  319.8 3.5 all-to-all-start.3
  323.6 12.3 %collective-permute-start.1 = (f32[4,1024]{1,0:T(4,128)S(1)}, f32[4,1024]{1,0:T(4,128)S(1)}, u32[]{:S(2)}, u32[]{:S(2)}) collective-permute-start(f32[4,1024]{1,0:T(4,128)S(1)} %convolution_multiply_fusion), channel_id=1, source_target_pairs={{8,0},{16,8},{24,16},{32,24},{40,32},{48,40},{56,48},{64,56},{72,6... | collective-permute-start | bytes 49160 | tf_op jit(solution)/shard_map/ppermute | solution.py:16
  336.3 101.2 %psum.7 = f32[1024,8]{0,1:T(8,128)} all-reduce(f32[1024,8]{0,1:T(8,128)S(1)} %convolution_bitcast_fusion), channel_id=1, replica_groups=mesh['dp'=64,'expert'=8] {'dp','expert'}, use_global_device_ids=true, to_apply=%region_10.11 | all-reduce | flops 8192 | bytes 65536 | tf_op jit(solution)/shard_map/psum | solution.py:124
  437.8 0.7 fusion.60
  438.5 1.2 gather_fusion.1
  439.7 1.5 fusion.30
  (39 shorter events, 3.4 us)
Async XLA Ops:
  7.2 22.6 %copy-start = (bf16[1024,8]{0,1:T(8,128)(2,1)S(1)}, bf16[1024,8]{0,1:T(8,128)(2,1)}, u32[]{:S(2)}) copy-start(bf16[1024,8]{0,1:T(8,128)(2,1)} %param.10) | copy-start | bytes 49156
  7.2 132.4 %all-gather.3.cloned.1.call-start = ((), (), s32[]{:S(2)}) async-start(), calls=%async_computation.4 | async-start | bytes 4259840 | tf_op jit(solution)/shard_map/all_gather | solution.py:65
  7.9 255.0 %all-gather.5.cloned.1.call-start = ((), (), s32[]{:S(2)}) async-start(), calls=%async_computation.5 | async-start | bytes 4259840 | tf_op jit(solution)/shard_map/all_gather | solution.py:66
  12.5 28.9 %all-to-all-start = ((bf16[8,40,1024]{2,1,0:T(8,128)(2,1)}), bf16[8,40,1024]{2,1,0:T(8,128)(2,1)S(1)}, u32[]{:S(2)}, u32[]{:S(2)}) async-start(bf16[8,40,1024]{2,1,0:T(8,128)(2,1)} %bitcast), calls=%async_computation | async-start | bytes 1310720 | tf_op jit(solution)/shard_map/all_to_all | solution.py:54
  25.7 249.9 %collective-permute-start = (bf16[4,1024]{1,0:T(4,128)(2,1)}, bf16[4,1024]{1,0:T(4,128)(2,1)S(1)}, u32[]{:S(2)}, u32[]{:S(2)}) collective-permute-start(bf16[4,1024]{1,0:T(4,128)(2,1)} %param.13), channel_id=1, source_target_pairs={{504,0},{0,8},{8,16},{16,24},{24,32},{32,40},{40,48},{48,56},{56,6... | collective-permute-start | bytes 24584 | tf_op jit(solution)/shard_map/ppermute | solution.py:16
  143.3 124.4 %copy-start.5 = (f32[320,2048]{1,0:T(8,128)}, f32[320,2048]{1,0:T(8,128)S(1)}, u32[]{:S(2)}) copy-start(f32[320,2048]{1,0:T(8,128)S(1)} %fusion.6) | copy-start | bytes 7864324
  143.4 131.9 %copy-start.2 = (bf16[4,1024]{1,0:T(4,128)(2,1)S(1)}, bf16[4,1024]{1,0:T(4,128)(2,1)}, u32[]{:S(2)}) copy-start(bf16[4,1024]{1,0:T(4,128)(2,1)} %param.13) | copy-start | bytes 24580
  143.4 132.0 %copy-start.4 = (s32[256]{0:T(256)S(1)}, s32[256]{0:T(256)}, u32[]{:S(2)}) copy-start(s32[256]{0:T(256)} %param.9) | copy-start | bytes 3076
  267.8 23.6 %all-to-all-start.1 = ((bf16[8,40,1024]{2,1,0:T(8,128)(2,1)}), bf16[8,40,1024]{2,1,0:T(8,128)(2,1)S(1)}, u32[]{:S(2)}, u32[]{:S(2)}) async-start(bf16[8,40,1024]{2,1,0:T(8,128)(2,1)} %bitcast.4), calls=%async_computation.1 | async-start | bytes 1310720 | tf_op jit(solution)/shard_map/all_to_all | solution.py:75
  311.1 24.9 %copy-start.1 = (bf16[256,1024]{1,0:T(8,128)(2,1)S(1)}, bf16[256,1024]{1,0:T(8,128)(2,1)}, u32[]{:S(2)}) copy-start(bf16[256,1024]{1,0:T(8,128)(2,1)} %param.7) | copy-start | bytes 1572868
  311.1 24.9 %copy-start.3 = (s32[256]{0:T(256)S(1)}, s32[256]{0:T(256)}, u32[]{:S(2)}) copy-start(s32[256]{0:T(256)} %param.8) | copy-start | bytes 3076
  319.8 118.7 %all-to-all-start.3 = ((bf16[8,40,1024]{2,1,0:T(8,128)(2,1)}), bf16[8,40,1024]{2,1,0:T(8,128)(2,1)S(1)}, u32[]{:S(2)}, u32[]{:S(2)}) async-start(bf16[8,40,1024]{2,1,0:T(8,128)(2,1)} %bitcast.10), calls=%async_computation.3 | async-start | bytes 1310720 | tf_op jit(solution)/shard_map/all_to_all | solution.py:137
  323.6 113.9 %collective-permute-start.1 = (f32[4,1024]{1,0:T(4,128)S(1)}, f32[4,1024]{1,0:T(4,128)S(1)}, u32[]{:S(2)}, u32[]{:S(2)}) collective-permute-start(f32[4,1024]{1,0:T(4,128)S(1)} %convolution_multiply_fusion), channel_id=1, source_target_pairs={{8,0},{16,8},{24,16},{32,24},{40,32},{48,40},{56,48},{64,56},{72,6... | collective-permute-start | bytes 49160 | tf_op jit(solution)/shard_map/ppermute | solution.py:16
Sparse Core Ops, SparseCore 0:
  10.1 129.4 all-gather.2
  141.8 121.0 all-gather.4
where the time goes:
time: 449 us; the launch traced here: 448 us
  waiting for transfers between devices  245 us (55%)
  blocking collectives  116 us (26%)
  starting transfers between devices  40.8 us (9%)
  matrix products  22.1 us (5%)
  between operations  14.2 us (3%)
  local copies, waits for them, and re-layouts  7.48 us (2%)
    all_gather x1, waiting for transfers between devices, body(): lax.all_gather(w_out, 'dp', axis=2, tiled=True)  120 us
    psum x1, blocking collectives, body(): router_grad = lax.psum(partial_value, ('dp', 'expert'))  101 us
    all_gather x1, waiting for transfers between devices, body(): lax.all_gather(w_in, 'dp', axis=1, tiled=True)  98.3 us
    ppermute x2, starting transfers between devices, shifted(): return lax.ppermute(block, axis, route)  16.4 us
    all_to_all x1, waiting for transfers between devices, body(): lax.all_to_all(expert_out.reshape(sources, capacity, model_width), 'exper...  15.6 us
    all_to_all x1, blocking collectives, body(): lax.all_to_all(grad_buffer.reshape(experts, capacity, model_width), 'expe...  14.7 us
    all_to_all x1, starting transfers between devices, body(): lax.all_to_all(send_buffer.reshape(experts, capacity, model_width), 'expe...  13.3 us
    all_to_all x1, waiting for transfers between devices, body(): lax.all_to_all(send_buffer.reshape(experts, capacity, model_width), 'expe...  10.3 us
  transfers between devices with their start and end apart: 7, of which 4 were waited for; matrix products, arithmetic and copies ran while one was open for 4% of the time, Pallas kernels for 0%

commit v1 on v0

--- a/solution.py
+++ b/solution.py
@@ -121,7 +121,7 @@
     grad_gate = jnp.sum(grad_branch * combined, axis=1)
     grad_logits = chosen * (grad_gate * gate_values * (1.0 - gate_values) * kept_float)[:, None]
     partial_value = jnp.dot(tokens.astype(jnp.float32).T, grad_logits, precision=highest)
-    router_grad = lax.psum(partial_value, ("dp", "expert"))
+    router_grad = jnp.sum(lax.all_gather(partial_value, ("dp", "expert")), axis=0)
     router_part = jnp.dot(grad_logits, router.astype(jnp.float32).T, precision=highest)
     grads_in = lax.all_to_all(
         grad_buffer.reshape(experts, capacity, model_width),

time: 449 us -> 1760 us (3.92)
  waiting for transfers between devices: 245 us -> 1650 us
  blocking collectives: 116 us -> 14.7 us
    all_gather x0 -> x1, waiting for transfers between devices: none -> 1400 us  [body(): lax.all_gather(partial_value, ('dp', 'expert'))]
    psum x1 -> x0, blocking collectives: 101 us -> none  [body(): router_grad = lax.psum(partial_value, ('dp', 'expert'))]
  transfers between devices with their start and end apart: 7 -> 8, of which waited for: 4 -> 6; matrix products, arithmetic and copies ran while one was open for 4% -> 2% of each run, Pallas kernels for 0% -> 0%
where the time goes in v1:
time: 1760 us
  waiting for transfers between devices  1650 us (94%)
  starting transfers between devices  40.9 us (2%)
  matrix products  22.6 us (1%)
    all_gather x1, waiting for transfers between devices, body(): lax.all_gather(partial_value, ('dp', 'expert'))  1400 us
    all_gather x1, waiting for transfers between devices, body(): lax.all_gather(w_out, 'dp', axis=2, tiled=True)  120 us
    all_gather x1, waiting for transfers between devices, body(): lax.all_gather(w_in, 'dp', axis=1, tiled=True)  98.2 us
  transfers between devices with their start and end apart: 8, of which 6 were waited for; matrix products, arithmetic and copies ran while one was open for 2% of the time, Pallas kernels for 0%

profile of v1, /device:TPU:1, one launch (start us, length us, event | category | flops | bytes accessed | tf_op | source)
XLA Modules:
  0.0 1759.2 jit_solution(18202166920562824703)
XLA Ops:
  8.7 0.7 compare_select_fusion
  9.4 3.0 scatter_custom_fusion
  12.4 13.3 all-to-all-start
  25.7 4.0 collective-permute-start
  29.7 1.3 fusion.33
  31.1 10.3 all-to-all-done
  41.3 98.2 %all-gather.5.cloned.1.call-done = bf16[1,1024,2048]{2,1,0:T(8,128)(2,1)} async-done(((bf16[1,16,2048]{2,1,0:T(8,128)(2,1)}), bf16[1,1024,2048]{2,1,0:T(8,128)(2,1)}) %all-gather.5.cloned.1.call-update) | async-done | bytes 4194320 | tf_op jit(solution)/shard_map/all_gather | solution.py:65
  139.5 3.7 fusion.6
  143.3 119.6 %all-gather.7.cloned.1.call-done = bf16[1,2048,1024]{1,2,0:T(8,128)(2,1)} async-done(((bf16[1,2048,16]{1,2,0:T(8,128)(2,1)}), bf16[1,2048,1024]{1,2,0:T(8,128)(2,1)}) %all-gather.7.cloned.1.call-update) | async-done | bytes 4194320 | tf_op jit(solution)/shard_map/all_gather | solution.py:66
  262.8 4.8 fusion.23
  267.6 7.5 all-to-all-start.1
  275.7 15.5 all-to-all-done.1
  291.2 1.2 gather_fusion
  294.3 0.9 convolution_bitcast_fusion
  295.3 1.9 scatter_custom_fusion.1
  297.2 14.7 all_to_all.20
  311.9 8.7 fusion.20
  320.6 3.5 all-to-all-start.3
  324.4 12.4 collective-permute-start.1
  336.8 2.7 collective-permute-done.1
  340.6 1.2 gather_fusion.1
  341.7 1.5 fusion.30
  343.2 1402.1 %all-gather.9.cloned.1.call-done = f32[524288,8]{0,1:T(8,128)} async-done(((f32[1024,8]{0,1:T(8,128)}), f32[524288,8]{0,1:T(8,128)}) %all-gather.9.cloned.1.call-update) | async-done | bytes 16777232 | tf_op jit(solution)/shard_map/all_gather | solution.py:124
  1745.3 7.4 reduce_sum.89
  (42 shorter events, 5.2 us)
Async XLA Ops:
  7.2 22.6 %copy-start = (bf16[1024,8]{0,1:T(8,128)(2,1)S(1)}, bf16[1024,8]{0,1:T(8,128)(2,1)}, u32[]{:S(2)}) copy-start(bf16[1024,8]{0,1:T(8,128)(2,1)} %param.10) | copy-start | bytes 49156
  7.2 132.3 %all-gather.5.cloned.1.call-start = ((), (), s32[]{:S(2)}) async-start(), calls=%async_computation.4 | async-start | bytes 4259840 | tf_op jit(solution)/shard_map/all_gather | solution.py:65
  7.9 254.9 %all-gather.7.cloned.1.call-start = ((), (), s32[]{:S(2)}) async-start(), calls=%async_computation.5 | async-start | bytes 4259840 | tf_op jit(solution)/shard_map/all_gather | solution.py:66
  12.4 28.9 %all-to-all-start = ((bf16[8,40,1024]{2,1,0:T(8,128)(2,1)}), bf16[8,40,1024]{2,1,0:T(8,128)(2,1)S(1)}, u32[]{:S(2)}, u32[]{:S(2)}) async-start(bf16[8,40,1024]{2,1,0:T(8,128)(2,1)} %bitcast), calls=%async_computation | async-start | bytes 1310720 | tf_op jit(solution)/shard_map/all_to_all | solution.py:54
  25.7 249.8 %collective-permute-start = (bf16[4,1024]{1,0:T(4,128)(2,1)}, bf16[4,1024]{1,0:T(4,128)(2,1)S(1)}, u32[]{:S(2)}, u32[]{:S(2)}) collective-permute-start(bf16[4,1024]{1,0:T(4,128)(2,1)} %param.13), channel_id=1, source_target_pairs={{504,0},{0,8},{8,16},{16,24},{24,32},{32,40},{40,48},{48,56},{56,6... | collective-permute-start | bytes 24584 | tf_op jit(solution)/shard_map/ppermute | solution.py:16
  143.2 124.4 %copy-start.5 = (f32[320,2048]{1,0:T(8,128)}, f32[320,2048]{1,0:T(8,128)S(1)}, u32[]{:S(2)}) copy-start(f32[320,2048]{1,0:T(8,128)S(1)} %fusion.6) | copy-start | bytes 7864324
  143.2 131.9 %copy-start.2 = (bf16[4,1024]{1,0:T(4,128)(2,1)S(1)}, bf16[4,1024]{1,0:T(4,128)(2,1)}, u32[]{:S(2)}) copy-start(bf16[4,1024]{1,0:T(4,128)(2,1)} %param.13) | copy-start | bytes 24580
  143.2 132.1 %copy-start.4 = (s32[256]{0:T(256)S(1)}, s32[256]{0:T(256)}, u32[]{:S(2)}) copy-start(s32[256]{0:T(256)} %param.9) | copy-start | bytes 3076
  267.6 23.6 %all-to-all-start.1 = ((bf16[8,40,1024]{2,1,0:T(8,128)(2,1)}), bf16[8,40,1024]{2,1,0:T(8,128)(2,1)S(1)}, u32[]{:S(2)}, u32[]{:S(2)}) async-start(bf16[8,40,1024]{2,1,0:T(8,128)(2,1)} %bitcast.4), calls=%async_computation.1 | async-start | bytes 1310720 | tf_op jit(solution)/shard_map/all_to_all | solution.py:75
  275.1 1470.2 %all-gather.9.cloned.1.call-start = ((), (), s32[]{:S(2)}) async-start(), calls=%async_computation.6 | async-start | bytes 16809984 | tf_op jit(solution)/shard_map/all_gather | solution.py:124
  291.2 3.1 copy-start.1
  291.2 3.1 copy-start.3
  320.6 20.0 %all-to-all-start.3 = ((bf16[8,40,1024]{2,1,0:T(8,128)(2,1)}), bf16[8,40,1024]{2,1,0:T(8,128)(2,1)S(1)}, u32[]{:S(2)}, u32[]{:S(2)}) async-start(bf16[8,40,1024]{2,1,0:T(8,128)(2,1)} %bitcast.10), calls=%async_computation.3 | async-start | bytes 1310720 | tf_op jit(solution)/shard_map/all_to_all | solution.py:137
  324.4 15.1 collective-permute-start.1
Sparse Core Ops, SparseCore 0:
  10.1 129.3 all-gather.4
  141.7 121.1 all-gather.6
  295.4 1449.8 all-gather.8
